TPU v7x, 32 devices: a whole 2x2x4 slice. The times are simulated.
32 devices in a mesh: dp: 8 (over y, x, core), shard: 4 (over z).
Axes of the slice: x: 2, y: 2, z: 4, core: 2. Of those that a mesh axis runs over, the one named last changes fastest.
Arguments:
- activations: bfloat16 [4096, 4096], P('dp', 'shard'), may hold values from -6 to 6
- out_grads: bfloat16 [4096, 14336], P('dp', 'shard'), may hold values from -6 to 6
- sign_bits: int32 [14336], P('shard'), may hold values from 0 to 1
- block_ids: int32 [4, 8], replicated, may hold values from 0 to 111, as said below
Outputs:
- gram: float32 [4096, 1024], P('shard')
Inputs may be any that keep to these rules, and one draw needn't show every extreme that they name: `block_ids`: row o holds 4 runs of 2 entries; the entries of a run are distinct blocks of one shard s (ids s * 28 + 0 to s * 28 + 27), and the runs of a row come from distinct shards.
All inputs are finite; a program needn't handle non-finite values.
Results may differ from a plain program's by a relative error of at most 0.006.
Values may be sent and summed in bfloat16 or wider, within the bound.
A program may use at most 64 MiB of HBM per device.

v0:
```python
import math
import jax
import jax.numpy as jnp
from jax import lax
from jax.sharding import PartitionSpec as P

BLK = 128
CAP = 2


def partner_2(x, axis, distance):
    return lax.ppermute(x, axis, [(i, i ^ 1 << distance) for i in range(lax.axis_size(axis))])


def parity_table(count):
    index = jnp.arange(count, dtype=jnp.int32)
    total = jnp.zeros((count, count), jnp.int32)
    for level in range(count.bit_length() - 1):
        total = total + (
            jnp.right_shift(index[:, None], level) & jnp.right_shift(index[None, :], level) & 1
        )
    return (1 - 2 * (total % 2)).astype(jnp.float32)


def route_sampled(mixed, block_ids, me_index, shards, blocks_per, tokens, width):
    groups = block_ids.shape[1] // CAP
    sources = block_ids[:, ::CAP] // blocks_per
    local_ids = (block_ids % blocks_per).reshape(shards, groups, CAP)
    matched = sources == me_index
    chosen = jnp.sum(jnp.where(matched[:, :, None], local_ids, 0), axis=1)
    live_rows = jnp.any(matched, axis=1).astype(jnp.bfloat16)
    outgoing = jnp.take(mixed, chosen.reshape(-1), axis=0).reshape(shards, CAP, tokens, width)
    return (outgoing * live_rows[:, None, None, None], jnp.take(sources, me_index, axis=0))


def body(activations, out_grads, sign_bits, block_ids):
    shards = lax.axis_size("shard")
    me_index = lax.axis_index("shard")
    tokens = out_grads.shape[0]
    width = BLK
    own_blocks = block_ids.shape[1]
    blocks_per = out_grads.shape[1] // width
    model_width = activations.shape[1] * shards
    inv_block = 1.0 / math.sqrt(width)
    inv_shard = 1.0 / math.sqrt(shards)
    partial_gram = jnp.dot(activations, activations.T, preferred_element_type=jnp.float32)
    token_gram = lax.psum(partial_gram, "shard").astype(jnp.bfloat16)
    sign_values = (1 - 2 * sign_bits).astype(jnp.bfloat16)
    flipped = (out_grads * sign_values[None, :]).reshape(tokens, blocks_per, width)
    block_table = parity_table(width).astype(jnp.bfloat16)
    local_mix = jnp.einsum("tbj,jk->btk", flipped, block_table, preferred_element_type=jnp.float32)
    local_mix = (local_mix * inv_block).astype(jnp.bfloat16)
    running = local_mix.astype(jnp.float32)
    for level in range(shards.bit_length() - 1):
        partner = partner_2(running, "shard", level)
        upper = jnp.right_shift(me_index, level) & 1 == 1
        running = jnp.where(upper, partner - running, running + partner)
    mixed = (running * inv_shard).astype(jnp.bfloat16)
    outgoing, own_sources = route_sampled(
        mixed, block_ids, me_index, shards, blocks_per, tokens, width
    )
    incoming = lax.all_to_all(outgoing, "shard", split_axis=0, concat_axis=0, tiled=True)
    sketched = jnp.take(incoming, own_sources, axis=0).reshape(own_blocks, tokens, width)
    weighted = jnp.einsum(
        "tu,jub->jtb", token_gram, sketched, preferred_element_type=jnp.float32
    ).astype(jnp.bfloat16)
    block_gram = jnp.einsum("jtb,ktc->jbkc", sketched, weighted, preferred_element_type=jnp.float32)
    own_cols = own_blocks * width
    block_gram = block_gram.reshape(own_cols, own_cols)
    summed = lax.psum(block_gram, "dp")
    return summed / (lax.axis_size("dp") * tokens * model_width)


def solution(mesh):
    in_specs = (P("dp", "shard"), P("dp", "shard"), P("shard"), P())
    out_specs = P("shard", None)
    return jax.shard_map(body, mesh=mesh, in_specs=in_specs, out_specs=out_specs, check_vma=False)
```

profile of v0, /device:TPU:0, one launch (start us, length us, event | category | flops | bytes accessed | tf_op | source)
XLA Modules:
  0.0 690.9 jit_solution(8151458818415333310)
XLA Ops:
  6.6 6.0 copy.15
  12.6 0.0 copy-done.1
  12.6 3.3 broadcast_multiply_fusion.1
  15.9 4.3 convert_bitcast_fusion
  20.2 3.1 collective-permute-start
  23.3 158.3 %collective-permute-done = f32[28,512,128]{1,2,0:T(8,128)} collective-permute-done((f32[28,512,128]{1,2,0:T(8,128)}, f32[28,512,128]{1,2,0:T(8,128)}, u32[]{:S(2)}, u32[]{:S(2)}) %collective-permute-start) | collective-permute-done | bytes 7340064 | tf_op jit(solution)/shard_map/ppermute | solution.py:12
  181.6 10.6 %add_select_fusion = f32[28,512,128]{1,2,0:T(8,128)} fusion(f32[28,512,128]{1,2,0:T(8,128)} %convert_bitcast_fusion, f32[28,512,128]{1,2,0:T(8,128)} %collective-permute-done, pred[]{:T(512)S(6)} %eq.19), kind=kLoop, calls=%fused_computation.4 | loop fusion | flops 5505024 | bytes 22020096 | tf_op jit(solution)/shard_map/jit(_where)/select_n | solution.py:57
  192.1 2.8 collective-permute-start.1
  194.9 0.1 slice.3
  195.0 0.1 copy.13
  195.1 0.1 fusion.32
  195.2 0.1 copy.12
  195.3 0.1 copy.17
  195.4 0.1 reshape.154
  195.5 0.1 copy.14
  195.7 0.1 broadcast_in_dim.63
  195.7 0.1 broadcast_in_dim.64
  195.8 314.0 %collective-permute-done.1 = f32[28,512,128]{1,2,0:T(8,128)} collective-permute-done((f32[28,512,128]{1,2,0:T(8,128)}, f32[28,512,128]{1,2,0:T(8,128)}, u32[]{:S(2)}, u32[]{:S(2)}) %collective-permute-start.1) | collective-permute-done | bytes 7340064 | tf_op jit(solution)/shard_map/ppermute | solution.py:12
  509.8 9.1 %multiply_convert_fusion = bf16[28,512,128]{1,2,0:T(8,128)(2,1)} fusion(f32[28,512,128]{1,2,0:T(8,128)} %add_select_fusion, f32[28,512,128]{1,2,0:T(8,128)} %collective-permute-done.1, pred[]{:T(512)S(6)} %eq.18), kind=kLoop, calls=%fused_computation.3 | loop fusion | flops 9175040 | bytes 18350080 | tf_op jit(solution)/shard_map/convert_element_type | solution.py:58
  518.9 2.6 gather_fusion
  521.5 1.1 select_multiply_fusion
  522.7 4.6 all-to-all-start
  527.3 0.7 fusion.33
  528.1 63.9 %all-reduce.4 = bf16[512,512]{1,0:T(8,128)(2,1)} all-reduce(f32[512,512]{1,0:T(8,128)S(1)} %fusion.33), channel_id=1, replica_groups=mesh['dp'=8,'shard'=4] {'shard'}, use_global_device_ids=true, to_apply=%region_2.3 | all-reduce | flops 262144 | bytes 1572864 | tf_op jit(solution)/shard_map/psum | solution.py:47
  591.9 0.0 all-to-all-done
  591.9 0.6 gather_fusion.1
  592.6 0.2 bitcast_select_fusion
  592.7 1.8 convolution_convert_fusion
  594.5 3.3 fusion.34
  597.8 0.0 all-reduce.3.cloned.1.call-update
  597.8 81.2 %all-reduce.3.cloned.1.call-done = f32[1024,1024]{1,0:T(8,128)} async-done(((f32[1024,1024]{1,0:T(8,128)}), f32[1024,1024]{1,0:T(8,128)}) %all-reduce.3.cloned.1.call-update) | async-done | bytes 4194320 | tf_op jit(solution)/shard_map/psum | solution.py:70
  679.0 5.0 broadcast_multiply_fusion
  (20 shorter events, 0.1 us)
Async XLA Ops:
  6.5 520.8 %copy-start = (bf16[512,1024]{1,0:T(8,128)(2,1)S(1)}, bf16[512,1024]{1,0:T(8,128)(2,1)}, u32[]{:S(2)}) copy-start(bf16[512,1024]{1,0:T(8,128)(2,1)} %param.4) | copy-start | bytes 3145732
  6.5 6.0 copy-start.1
  20.2 161.4 %collective-permute-start = (f32[28,512,128]{1,2,0:T(8,128)}, f32[28,512,128]{1,2,0:T(8,128)}, u32[]{:S(2)}, u32[]{:S(2)}) collective-permute-start(f32[28,512,128]{1,2,0:T(8,128)} %convert_bitcast_fusion), channel_id=1, source_target_pairs={{0,1},{1,0},{2,3},{3,2},{4,5},{5,4},{6,7},{7,6},{8,9},{9,8},{10,11... | collective-permute-start | bytes 22020104 | tf_op jit(solution)/shard_map/ppermute | solution.py:12
  23.3 171.6 %copy-start.2 = (s32[4,8]{1,0:T(4,128)S(1)}, s32[4,8]{1,0:T(4,128)}, u32[]{:S(2)}) copy-start(s32[4,8]{1,0:T(4,128)} %param.7) | copy-start | bytes 388
  192.1 317.7 %collective-permute-start.1 = (f32[28,512,128]{1,2,0:T(8,128)}, f32[28,512,128]{1,2,0:T(8,128)}, u32[]{:S(2)}, u32[]{:S(2)}) collective-permute-start(f32[28,512,128]{1,2,0:T(8,128)} %add_select_fusion), channel_id=1, source_target_pairs={{0,2},{1,3},{2,0},{3,1},{4,6},{5,7},{6,4},{7,5},{8,10},{9,11},{10,... | collective-permute-start | bytes 22020104 | tf_op jit(solution)/shard_map/ppermute | solution.py:12
  522.7 69.3 %all-to-all-start = ((bf16[4,2,512,128]{2,3,1,0:T(8,128)(2,1)}), bf16[4,2,512,128]{2,3,1,0:T(8,128)(2,1)S(1)}, u32[]{:S(2)}, u32[]{:S(2)}) async-start(bf16[4,2,512,128]{2,3,1,0:T(8,128)(2,1)} %select_multiply_fusion), calls=%async_computation | async-start | bytes 2097152 | tf_op jit(solution)/shard_map/all_to_all | solution.py:62
  527.3 151.7 %all-reduce.3.cloned.1.call-start = ((), (), s32[]{:S(2)}) async-start(), calls=%async_computation.1 | async-start | bytes 8388608 | tf_op jit(solution)/shard_map/psum | solution.py:70
Sparse Core Ops, SparseCore 0:
  598.0 80.9 all-reduce.2
where the time goes:
time: 691 us
  waiting for transfers between devices  553 us (80%)
  blocking collectives  63.9 us (9%)
  other arithmetic  29.5 us (4%)
  between operations  13.5 us (2%)
  starting transfers between devices  10.5 us (2%)
  matrix products  10.1 us (1%)
  local copies, waits for them, and re-layouts  10 us (1%)
    ppermute x2, waiting for transfers between devices, partner_2(): lax.ppermute(x, axis, [(i, i ^ 1 << distance) for i in range(lax.axis_siz...  472 us
    psum x1, waiting for transfers between devices, body(): summed = lax.psum(block_gram, 'dp')  81.2 us
    psum x1, blocking collectives, body(): token_gram = lax.psum(partial_gram, 'shard').astype(jnp.bfloat16)  63.9 us
  transfers between devices with their start and end apart: 4, of which 3 were waited for; matrix products, arithmetic and copies ran while one was open for 0% of the time, Pallas kernels for 0%

commit v1 on v0

--- a/solution.py
+++ b/solution.py
@@ -67,7 +67,8 @@
     block_gram = jnp.einsum("jtb,ktc->jbkc", sketched, weighted, preferred_element_type=jnp.float32)
     own_cols = own_blocks * width
     block_gram = block_gram.reshape(own_cols, own_cols)
-    summed = lax.psum(block_gram, "dp")
+    shards_2 = lax.all_gather(block_gram, "dp", axis=0, tiled=False)
+    summed = shards_2.sum(axis=0)
     return summed / (lax.axis_size("dp") * tokens * model_width)
 
 

time: 691 us -> 786 us (1.14)
  waiting for transfers between devices: 553 us -> 633 us
  other arithmetic: 29.5 us -> 45 us
    all_gather x0 -> x1, waiting for transfers between devices: none -> 161 us  [body(): shards_2 = lax.all_gather(block_gram, 'dp', axis=0, tiled=False)]
    psum x1 -> x0, waiting for transfers between devices: 81.2 us -> none  [body(): summed = lax.psum(block_gram, 'dp')]
    reduce_sum x0 -> x1, other arithmetic: none -> 14.7 us  [body(): summed = shards_2.sum(axis=0)]
where the time goes in v1:
time: 786 us; the launch traced here: 785 us
  waiting for transfers between devices  633 us (81%)
  blocking collectives  63.8 us (8%)
  other arithmetic  45 us (6%)
  between operations  13.5 us (2%)
  starting transfers between devices  10.5 us (1%)
  local copies, waits for them, and re-layouts  10.2 us (1%)
  matrix products  9.05 us (1%)
    ppermute x2, waiting for transfers between devices, partner_2(): lax.ppermute(x, axis, [(i, i ^ 1 << distance) for i in range(lax.axis_siz...  472 us
    all_gather x1, waiting for transfers between devices, body(): shards_2 = lax.all_gather(block_gram, 'dp', axis=0, tiled=False)  161 us
    psum x1, blocking collectives, body(): token_gram = lax.psum(partial_gram, 'shard').astype(jnp.bfloat16)  63.8 us
  transfers between devices with their start and end apart: 4, of which 3 were waited for; matrix products, arithmetic and copies ran while one was open for 0% of the time, Pallas kernels for 0%

profile of v1, /device:TPU:0, one launch (start us, length us, event | category | flops | bytes accessed | tf_op | source)
XLA Modules:
  0.0 785.3 jit_solution(7929377771402737445)
XLA Ops:
  6.6 0.8 subtract_convert_fusion
  7.4 5.9 copy.15
  13.3 3.3 broadcast_multiply_fusion.1
  16.6 4.3 convert_bitcast_fusion
  20.9 3.1 collective-permute-start
  23.9 158.3 %collective-permute-done = f32[28,512,128]{1,2,0:T(8,128)} collective-permute-done((f32[28,512,128]{1,2,0:T(8,128)}, f32[28,512,128]{1,2,0:T(8,128)}, u32[]{:S(2)}, u32[]{:S(2)}) %collective-permute-start) | collective-permute-done | bytes 7340064 | tf_op jit(solution)/shard_map/ppermute | solution.py:12
  182.2 10.6 %add_select_fusion = f32[28,512,128]{1,2,0:T(8,128)} fusion(f32[28,512,128]{1,2,0:T(8,128)} %convert_bitcast_fusion, f32[28,512,128]{1,2,0:T(8,128)} %collective-permute-done, pred[]{:T(512)S(6)} %eq.19), kind=kLoop, calls=%fused_computation.4 | loop fusion | flops 5505024 | bytes 22020096 | tf_op jit(solution)/shard_map/jit(_where)/select_n | solution.py:57
  192.8 2.8 collective-permute-start.1
  195.5 0.1 slice.3
  195.6 0.1 copy.13
  195.7 0.1 fusion.32
  195.9 0.1 copy.12
  196.0 0.1 broadcast_in_dim.63
  196.1 0.1 broadcast_in_dim.64
  196.2 0.1 copy.17
  196.3 0.1 copy.14
  196.4 0.1 reshape.158
  196.5 313.9 %collective-permute-done.1 = f32[28,512,128]{1,2,0:T(8,128)} collective-permute-done((f32[28,512,128]{1,2,0:T(8,128)}, f32[28,512,128]{1,2,0:T(8,128)}, u32[]{:S(2)}, u32[]{:S(2)}) %collective-permute-start.1) | collective-permute-done | bytes 7340064 | tf_op jit(solution)/shard_map/ppermute | solution.py:12
  510.4 9.1 %multiply_convert_fusion = bf16[28,512,128]{1,2,0:T(8,128)(2,1)} fusion(f32[28,512,128]{1,2,0:T(8,128)} %add_select_fusion, f32[28,512,128]{1,2,0:T(8,128)} %collective-permute-done.1, pred[]{:T(512)S(6)} %eq.18), kind=kLoop, calls=%fused_computation.3 | loop fusion | flops 9175040 | bytes 18350080 | tf_op jit(solution)/shard_map/convert_element_type | solution.py:58
  519.5 2.6 gather_fusion
  522.1 1.1 select_multiply_fusion
  523.3 4.6 all-to-all-start
  527.9 0.7 fusion.33
  528.7 63.8 %all-reduce.1 = bf16[512,512]{1,0:T(8,128)(2,1)} all-reduce(f32[512,512]{1,0:T(8,128)S(1)} %fusion.33), channel_id=1, replica_groups=mesh['dp'=8,'shard'=4] {'shard'}, use_global_device_ids=true, to_apply=%region_2.3 | all-reduce | flops 262144 | bytes 1572864 | tf_op jit(solution)/shard_map/psum | solution.py:47
  592.6 0.6 gather_fusion.1
  593.2 0.2 bitcast_select_fusion
  593.4 0.2 copy-done.2
  593.6 0.7 convolution_convert_fusion
  594.3 3.3 fusion.34
  597.7 161.0 %all-gather.3.cloned.1.call-done = f32[8192,1024]{1,0:T(8,128)} async-done(((f32[1024,1024]{1,0:T(8,128)}), f32[8192,1024]{1,0:T(8,128)}) %all-gather.3.cloned.1.call-update) | async-done | bytes 33554448 | tf_op jit(solution)/shard_map/all_gather | solution.py:70
  758.7 14.7 %reduce_sum.19 = f32[1024,1024]{1,0:T(8,128)} reduce(f32[8,1024,1024]{2,1,0:T(8,128)} %bitcast.32, f32[]{:T(128)} %constant.111.clone.1), dimensions={0}, to_apply=%region_3.4 | reduce | flops 7340032 | bytes 37748740 | tf_op jit(solution)/shard_map/reduce_sum | solution.py:71
  773.4 5.0 broadcast_multiply_fusion
  (23 shorter events, 0.1 us)
Async XLA Ops:
  6.5 521.4 %copy-start = (bf16[512,1024]{1,0:T(8,128)(2,1)S(1)}, bf16[512,1024]{1,0:T(8,128)(2,1)}, u32[]{:S(2)}) copy-start(bf16[512,1024]{1,0:T(8,128)(2,1)} %param.4) | copy-start | bytes 3145732
  20.9 161.3 %collective-permute-start = (f32[28,512,128]{1,2,0:T(8,128)}, f32[28,512,128]{1,2,0:T(8,128)}, u32[]{:S(2)}, u32[]{:S(2)}) collective-permute-start(f32[28,512,128]{1,2,0:T(8,128)} %convert_bitcast_fusion), channel_id=1, source_target_pairs={{0,1},{1,0},{2,3},{3,2},{4,5},{5,4},{6,7},{7,6},{8,9},{9,8},{10,11... | collective-permute-start | bytes 22020104 | tf_op jit(solution)/shard_map/ppermute | solution.py:12
  23.9 171.6 %copy-start.3 = (s32[4,8]{1,0:T(4,128)S(1)}, s32[4,8]{1,0:T(4,128)}, u32[]{:S(2)}) copy-start(s32[4,8]{1,0:T(4,128)} %param.7) | copy-start | bytes 388
  192.8 317.7 %collective-permute-start.1 = (f32[28,512,128]{1,2,0:T(8,128)}, f32[28,512,128]{1,2,0:T(8,128)}, u32[]{:S(2)}, u32[]{:S(2)}) collective-permute-start(f32[28,512,128]{1,2,0:T(8,128)} %add_select_fusion), channel_id=1, source_target_pairs={{0,2},{1,3},{2,0},{3,1},{4,6},{5,7},{6,4},{7,5},{8,10},{9,11},{10,... | collective-permute-start | bytes 22020104 | tf_op jit(solution)/shard_map/ppermute | solution.py:12
  523.3 69.3 %all-to-all-start = ((bf16[4,2,512,128]{2,3,1,0:T(8,128)(2,1)}), bf16[4,2,512,128]{2,3,1,0:T(8,128)(2,1)S(1)}, u32[]{:S(2)}, u32[]{:S(2)}) async-start(bf16[4,2,512,128]{2,3,1,0:T(8,128)(2,1)} %select_multiply_fusion), calls=%async_computation | async-start | bytes 2097152 | tf_op jit(solution)/shard_map/all_to_all | solution.py:62
  527.9 230.8 %all-gather.3.cloned.1.call-start = ((), (), s32[]{:S(2)}) async-start(), calls=%async_computation.1 | async-start | bytes 37748736 | tf_op jit(solution)/shard_map/all_gather | solution.py:70
  592.6 1.0 copy-start.2
  758.7 19.8 %copy-start.1 = (bf16[512,1024]{1,0:T(8,128)(2,1)S(1)}, bf16[512,1024]{1,0:T(8,128)(2,1)}, u32[]{:S(2)}) copy-start(bf16[512,1024]{1,0:T(8,128)(2,1)} %param.4) | copy-start | bytes 3145732
Sparse Core Ops, SparseCore 0:
  597.8 160.8 all-gather.2
